TPU v7x, 256 devices: a whole 4x4x8 slice. The times are simulated.
256 devices in a mesh: seq: 128 (over x, z, y), head: 2 (over core).
Axes of the slice: x: 4, y: 4, z: 8, core: 2. Of those that a mesh axis runs over, the one named last changes fastest.
Arguments:
- queries: bfloat16 [16384, 1024], P('seq', 'head'), may hold values from -6 to 6
- key_rows: bfloat16 [16384, 1024], P('seq', 'head'), may hold values from -6 to 6
- values: bfloat16 [16384, 2048], P('seq', 'head'), may hold values from -6 to 6
- out_gate: bfloat16 [16384, 2048], P('seq', 'head'), may hold values from -6 to 6
- write_rate: float32 [16, 16384], P('head', 'seq'), may hold values from 0 to 1
- log_decay: float32 [16, 16384], P('head', 'seq'), may hold values from -1 to 0, as said below
- norm_gain: float32 [128], replicated, may hold values from 0.1 to 1.9
- out_weight: bfloat16 [2048, 2048], P('head'), may hold values from -0.125 to 0.125
Outputs:
- layer_out: bfloat16 [16384, 2048], P('seq', 'head')
Inputs may be any that keep to these rules, and one draw needn't show every extreme that they name: `log_decay`: log decay of each value head and token, negative.
All inputs are finite; a program needn't handle non-finite values.
Results may differ from a plain program's by a relative error of at most 0.009.
Values may be sent and summed in bfloat16 or wider, within the bound.
A program may use at most 320 MiB of HBM per device.

v0:
```python
import jax
import jax.numpy as jnp
from jax import lax
from jax.sharding import PartitionSpec as P

DK = 128
DV = 128
SPAN = 64


epsilon = 1e-06
highest = lax.Precision.HIGHEST


def carried_in(value, axis, combine, identity):
    count, index = (lax.axis_size(axis), lax.axis_index(axis))
    everything = jax.tree.map(lambda part: lax.all_gather(part, axis), value)
    start = jax.tree.map(
        lambda part, zero: jnp.broadcast_to(jnp.asarray(zero, part.dtype), part.shape),
        value,
        identity,
    )

    def turn(k, before):
        reached = k < index
        new = combine(before, jax.tree.map(lambda part: part[k], everything))
        return jax.tree.map(lambda a, b: jnp.where(reached, a, b), new, before)

    return lax.fori_loop(0, count, turn, start)


def unit_rows(vectors):
    return vectors / jnp.sqrt(jnp.sum(vectors * vectors, axis=-1, keepdims=True) + epsilon)


def head_blocks(row_data, head_count, head_width, repeat, normalize):
    row_count = row_data.shape[0]
    vectors = row_data.astype(jnp.float32).reshape(row_count, head_count, head_width)
    if normalize:
        vectors = unit_rows(vectors)
    vectors = jnp.repeat(vectors, repeat, axis=1)
    return vectors.reshape(row_count // SPAN, SPAN, head_count * repeat, head_width).transpose(
        0, 2, 1, 3
    )


def block_terms(query_blk, key_blk, value_blk, rate_blk, decay_blk):
    length = query_blk.shape[-2]
    log_sums = jnp.cumsum(decay_blk, axis=-1)
    row_ids = lax.broadcasted_iota(jnp.int32, (length, length), 0)
    col_ids = lax.broadcasted_iota(jnp.int32, (length, length), 1)
    lower_mask = row_ids >= col_ids
    strict_mask = row_ids > col_ids
    log_gap = log_sums[..., :, None] - log_sums[..., None, :]
    decay_mat = jnp.where(lower_mask, jnp.exp(jnp.where(lower_mask, log_gap, 0.0)), 0.0)
    key_dots = jnp.einsum("...id,...jd->...ij", key_blk, key_blk, precision=highest)
    coupling = jnp.where(strict_mask, rate_blk[..., :, None] * key_dots * decay_mat, 0.0)
    scores = jnp.einsum("...id,...jd->...ij", query_blk, key_blk, precision=highest) * decay_mat
    growth = jnp.exp(log_sums)
    right_sides = jnp.concatenate(
        [rate_blk[..., None] * value_blk, (rate_blk * growth)[..., None] * key_blk], axis=-1
    )
    powered = coupling
    solved = right_sides - jnp.einsum("...ij,...jd->...id", powered, right_sides, precision=highest)
    for doubling in range(length.bit_length() - 2):
        powered = jnp.einsum("...ij,...jk->...ik", powered, powered, precision=highest)
        solved = solved + jnp.einsum("...ij,...jd->...id", powered, solved, precision=highest)
    value_width = value_blk.shape[-1]
    updates = solved[..., :value_width]
    weights = solved[..., value_width:]
    log_total = log_sums[..., -1:]
    key_decay = key_blk * jnp.exp(log_total - log_sums)[..., None]
    query_decay = query_blk * growth[..., None]
    keep_rate = jnp.exp(log_total)[..., None]
    return (updates, weights, scores, query_decay, key_decay, keep_rate)


def block_advance(memory, pieces):
    updates, weights, scores, query_decay, key_decay, keep_rate = pieces
    residue = updates - jnp.einsum("...cd,...de->...ce", weights, memory, precision=highest)
    output = jnp.einsum("...cd,...de->...ce", query_decay, memory, precision=highest) + jnp.einsum(
        "...ij,...je->...ie", scores, residue, precision=highest
    )
    memory = keep_rate * memory + jnp.einsum(
        "...cd,...ce->...de", key_decay, residue, precision=highest
    )
    return (memory, output)


def gated_norm(output, gate_vals, gain_row):
    inverse = lax.rsqrt(jnp.mean(output * output, axis=-1, keepdims=True) + epsilon)
    return (output * inverse * gain_row * jax.nn.silu(gate_vals)).astype(jnp.bfloat16)


def compose(running, block_pair):
    running_map, running_state = running
    block_map, block_feed = block_pair
    new_map = jnp.einsum("hij,hjk->hik", block_map, running_map, precision=highest)
    new_state = jnp.einsum("hij,hjk->hik", block_map, running_state, precision=highest) + block_feed
    return ((new_map, new_state), (running_map, running_state))


def combine(earlier, later_pair):
    joined_map = jnp.einsum("hij,hjk->hik", later_pair[0], earlier[0], precision=highest)
    joined_state = (
        jnp.einsum("hij,hjk->hik", later_pair[0], earlier[1], precision=highest) + later_pair[1]
    )
    return (joined_map, joined_state)


def per_device(queries, key_rows, values, out_gate, write_rate, log_decay, norm_gain, out_weight):
    tokens = queries.shape[0]
    value_heads = write_rate.shape[0]
    key_heads = queries.shape[1] // DK
    repeat = value_heads // key_heads
    blocks = tokens // SPAN
    query_blk = head_blocks(queries, key_heads, DK, repeat, True) * DK ** (-0.5)
    key_blk = head_blocks(key_rows, key_heads, DK, repeat, True)
    value_blk = head_blocks(values, value_heads, DV, 1, False)
    rate_blk = write_rate.reshape(value_heads, blocks, SPAN).transpose(1, 0, 2)
    decay_blk = log_decay.reshape(value_heads, blocks, SPAN).transpose(1, 0, 2)
    pieces = block_terms(query_blk, key_blk, value_blk, rate_blk, decay_blk)
    updates, weights, scores, query_decay, key_decay, keep_rate = pieces
    unit_matrix = jnp.eye(DK, dtype=jnp.float32)
    transition = keep_rate * unit_matrix - jnp.einsum(
        "...cd,...ce->...de", key_decay, weights, precision=highest
    )
    feed_state = jnp.einsum("...cd,...ce->...de", key_decay, updates, precision=highest)
    identity_map = jnp.broadcast_to(unit_matrix, (value_heads, DK, DK))
    zero_state = jnp.zeros((value_heads, DK, DV), jnp.float32)
    (total_map, total_state), (start_maps, start_states) = lax.scan(
        compose, (identity_map, zero_state), (transition, feed_state)
    )
    incoming = carried_in((total_map, total_state), "seq", combine, (identity_map, zero_state))
    entry_state = incoming[1]
    _, outputs = lax.scan(block_advance, entry_state, pieces)
    outputs = outputs.transpose(0, 2, 1, 3).reshape(tokens, value_heads, DV)
    gate_vals = out_gate.astype(jnp.float32).reshape(tokens, value_heads, DV)
    normed = gated_norm(outputs, gate_vals, norm_gain).reshape(tokens, value_heads * DV)
    partial_value = jnp.dot(normed, out_weight, preferred_element_type=jnp.float32)
    return lax.psum_scatter(
        partial_value.astype(jnp.bfloat16), "head", scatter_dimension=1, tiled=True
    )


def solution(mesh):
    return jax.shard_map(
        per_device,
        mesh=mesh,
        in_specs=(
            P("seq", "head"),
            P("seq", "head"),
            P("seq", "head"),
            P("seq", "head"),
            P("head", "seq"),
            P("head", "seq"),
            P(),
            P("head", None),
        ),
        out_specs=P("seq", "head"),
        check_vma=False,
    )
```

profile of v0, /device:TPU:1, one launch (start us, length us, event | category | flops | bytes accessed | tf_op | source)
XLA Modules:
  0.0 1000.9 jit_solution(8686059425483198752)
XLA Ops:
  22.6 3.0 fusion.57
  27.5 5.0 while.40
  36.3 2.0 convolution_multiply_fusion
  38.4 337.9 %all-gather.5.cloned.1.call-done = f32[1024,128,128]{2,1,0:T(8,128)} async-done(((f32[8,128,128]{2,1,0:T(8,128)}), f32[1024,128,128]{2,1,0:T(8,128)}) %all-gather.5.cloned.1.call-update) | async-done | bytes 67108880 | tf_op jit(solution)/shard_map/all_gather | solution.py:17
  376.3 340.4 %all-gather.7.cloned.1.call-done = f32[1024,128,128]{2,1,0:T(8,128)} async-done(((f32[8,128,128]{2,1,0:T(8,128)}), f32[1024,128,128]{2,1,0:T(8,128)}) %all-gather.7.cloned.1.call-update) | async-done | bytes 67108880 | tf_op jit(solution)/shard_map/all_gather | solution.py:17
  716.7 251.9 %while.41 = (s32[]{:T(128)}, f32[8,128,128]{2,1,0:T(8,128)S(1)}, s32[]{:T(128)}, f32[128,8,128,128]{3,2,1,0:T(8,128)}, f32[128,8,128,128]{3,2,1,0:T(8,128)}, /*index=5*/s32[]{:T(128)}, s32[]{:T(128)}) while((s32[]{:T(128)}, f32[8,128,128]{2,1,0:T(8,128)S(1)}, s32[]{:T(128)}, f32[128,8,128,128]{3,2,1,0:T(8,128)}, ...), condition=%wide.region_5.6_spmd.clone, body=%wide.region_4.5_spmd.clone.sunk | while | flops 201850880 | bytes 3672671 | solution.py:29
  718.7 1.9 fusion.132
  720.7 1.9 fusion.132
  726.6 1.9 fusion.132
  728.6 1.9 fusion.132
  730.5 1.9 fusion.132
  736.4 1.9 fusion.132
  754.1 1.9 fusion.132
  779.7 1.9 fusion.132
  805.3 1.9 fusion.132
  830.9 1.9 fusion.132
  856.5 1.9 fusion.132
  882.1 1.9 fusion.132
  907.6 1.9 fusion.132
  933.2 1.9 fusion.132
  958.8 1.9 fusion.132
  968.6 7.0 while.39
  978.5 3.9 convolution_convert_fusion
  982.4 12.0 %reduce-scatter.2.cloned.1.call-done = bf16[128,1024]{1,0:T(8,128)(2,1)} async-done(((bf16[128,2048]{1,0:T(8,128)(2,1)}), bf16[128,1024]{1,0:T(8,128)(2,1)}) %reduce-scatter.2.cloned.1.call-update) | async-done | bytes 262160 | tf_op jit(solution)/shard_map/reduce_scatter | solution.py:141
  (329 shorter events, 254.8 us)
Async XLA Ops:
  6.5 28.2 %copy-start = (f32[128]{0:T(128)S(1)}, f32[128]{0:T(128)}, u32[]{:S(2)}) copy-start(f32[128]{0:T(128)} %param.20) | copy-start | bytes 1540
  6.5 27.6 %copy-start.5 = (bf16[128,512]{1,0:T(8,128)(2,1)S(1)}, bf16[128,512]{1,0:T(8,128)(2,1)}, u32[]{:S(2)}) copy-start(bf16[128,512]{1,0:T(8,128)(2,1)} %param.14) | copy-start | bytes 393220
  6.5 971.9 %copy-start.6 = (bf16[128,1024]{1,0:T(8,128)(2,1)S(1)}, bf16[128,1024]{1,0:T(8,128)(2,1)}, u32[]{:S(2)}) copy-start(bf16[128,1024]{1,0:T(8,128)(2,1)} %param.17) | copy-start | bytes 786436
  6.5 369.7 %all-gather.5.cloned.1.call-start = ((), (), s32[]{:S(2)}) async-start(), calls=%async_computation.2 | async-start | bytes 67633152 | tf_op jit(solution)/shard_map/all_gather | solution.py:17
  11.5 8.3 copy-start.4
  22.6 3.0 copy-start.3
  32.5 0.8 copy-start.1
  32.5 1.0 copy-start.2
  33.3 683.4 %all-gather.7.cloned.1.call-start = ((), (), s32[]{:S(2)}) async-start(), calls=%async_computation.3 | async-start | bytes 67633152 | tf_op jit(solution)/shard_map/all_gather | solution.py:17
  34.1 960.3 %reduce-scatter.2.cloned.1.call-start = ((), (), s32[]{:S(2)}) async-start(), calls=%async_computation.1 | async-start | bytes 786432 | tf_op jit(solution)/shard_map/reduce_scatter | solution.py:141
Sparse Core Ops, SparseCore 0:
  33.5 342.7 all-gather.4
  379.9 336.7 all-gather.6
  982.5 11.8 reduce-scatter.1
where the time goes:
time: 1000 us
  waiting for transfers between devices  691 us (69%)
  matrix products  275 us (28%)
  between operations  13.5 us (1%)
  local copies, waits for them, and re-layouts  11.7 us (1%)
    all_gather x2, waiting for transfers between devices, carried_in(): everything = jax.tree.map(lambda part: lax.all_gather(part, axis), value)  678 us
    dot_general x128, matrix products, combine(): jnp.einsum('hij,hjk->hik', later_pair[0], earlier[1], precision=highest)  242 us
  transfers between devices with their start and end apart: 3, of which 3 were waited for; matrix products, arithmetic and copies ran while one was open for 0% of the time, Pallas kernels for 0%

commit v1 on v0

v1 whole, which is shorter than its diff:
```python
import jax
import jax.numpy as jnp
from jax import lax
from jax.experimental import pallas as pl
from jax.experimental.pallas import tpu as pltpu
from jax.sharding import PartitionSpec as P

HEAD_DIM = 128
TOKENS = 128
NX, NZ, NY = 4, 8, 4
EPS = 1e-06
F32, BF16 = jnp.float32, jnp.bfloat16
MESH = pl.DeviceIdType.MESH


def mm(a, b):
    return jnp.dot(a, b, preferred_element_type=F32)


def mm_nt(a, b):
    return lax.dot_general(a, b, (((1,), (1,)), ((), ())), preferred_element_type=F32)


def compose(later, earlier):
    return earlier + later - mm(later[:, HEAD_DIM:].astype(BF16), earlier.astype(BF16))


def advance(span, state):
    return state + span[:, :HEAD_DIM] - mm(span[:, HEAD_DIM:].astype(BF16), state.astype(BF16))


def kernel(
    q_ref, k_ref, v_ref, g_ref, wr_ref, ld_ref, gain_ref, w_hbm, out_ref,
    w_vm, uw, pm, qg, pu, gated, ysend, yg, zg, pairs, xsend, xg, sm, sin, nrm, psend, precv,
    wsem, ys_sem, yr_sem, zs_sem, zr_sem, xs_sem, xr_sem, bs_sem, br_sem, ps_sem, pr_sem,
):
    me, core = lax.axis_index("seq"), lax.axis_index("head")
    y = lax.rem(me, NY)
    z = lax.rem(lax.div(me, NY), NZ)
    x = lax.div(me, NY * NZ)

    def at(x_, z_, y_):
        return {"seq": (x_ * NZ + z_) * NY + y_}

    turns = (2, 1, 3)
    owners = [lax.rem(y + d, NY) for d in turns] + [y]
    y_peers = [at(x, z, owner) for owner in owners[:3]]
    x_peers = [at(lax.rem(x + d, NX), z, y) for d in turns]
    z_up, z_down = at(x, lax.rem(z + 1, NZ), y), at(x, lax.rem(z + NZ - 1, NZ), y)
    partner = {"head": 1 - core}

    barrier = pltpu.get_barrier_semaphore()
    for peer in y_peers + x_peers + [z_up, z_down, partner]:
        pl.semaphore_signal(barrier, inc=1, device_id=peer, device_id_type=MESH)
    weights = pltpu.make_async_copy(w_hbm, w_vm, wsem)
    weights.start()

    def remote(src, dst, send, recv, peer):
        return pltpu.make_async_remote_copy(
            src_ref=src, dst_ref=dst, send_sem=send, recv_sem=recv,
            device_id=peer, device_id_type=MESH,
        )

    rows = lax.broadcasted_iota(jnp.int32, (TOKENS, TOKENS), 0)
    cols = lax.broadcasted_iota(jnp.int32, (TOKENS, TOKENS), 1)
    apart = rows ^ cols
    lower, strict, diag = rows >= cols, rows > cols, rows == cols
    eye = jnp.where(diag, 1.0, 0.0).astype(F32)

    rate = jnp.concatenate([wr_ref[pl.ds(2 * p, 2), :] for p in owners], axis=0)
    decay = jnp.concatenate([ld_ref[pl.ds(2 * p, 2), :] for p in owners], axis=0)
    log_row = jnp.dot(
        decay, jnp.where(rows <= cols, 1.0, 0.0).astype(F32),
        precision=lax.Precision.HIGHEST, preferred_element_type=F32,
    )
    columns = jnp.concatenate([log_row, rate, jnp.zeros((TOKENS - 16, TOKENS), F32)], axis=0).T

    def terms(spots):
        units = []
        for i in spots:
            off = pl.multiple_of(owners[i] * HEAD_DIM, HEAD_DIM)
            kb, qb = k_ref[:, pl.ds(off, HEAD_DIM)], q_ref[:, pl.ds(off, HEAD_DIM)]
            kf, qf = kb.astype(F32), qb.astype(F32)
            dots = mm_nt(jnp.concatenate([kb, qb], axis=0), kb)
            key_dots, query_dots = dots[:TOKENS], dots[TOKENS:]
            key_row = lax.rsqrt(jnp.sum(jnp.where(diag, key_dots, 0.0), axis=0, keepdims=True) + EPS)
            key_col = lax.rsqrt(jnp.sum(kf * kf, axis=1, keepdims=True) + EPS)
            query_col = lax.rsqrt(jnp.sum(qf * qf, axis=1, keepdims=True) + EPS) * HEAD_DIM**-0.5
            key_dots, query_dots = key_dots * key_row, query_dots * key_row
            k_t = kf.T
            for e in range(2):
                j = 2 * i + e
                log_r, log_c = log_row[j : j + 1, :], columns[:, j : j + 1]
                rate_r, rate_c = rate[j : j + 1, :], columns[:, 8 + j : 9 + j]
                fade = jnp.exp(jnp.minimum(log_c - log_r, 0.0))
                grown = jnp.exp(log_c)
                coupling = jnp.where(strict, key_dots * fade * (rate_c * key_col), 0.0)
                pm[j] = jnp.where(lower, query_dots * fade * query_col, 0.0).astype(BF16)
                qg[j] = qf * (query_col * grown)
                v_off = pl.multiple_of(owners[i] * 2 * HEAD_DIM + e * HEAD_DIM, HEAD_DIM)
                right = jnp.concatenate(
                    [v_ref[:, pl.ds(v_off, HEAD_DIM)], (kf * (key_col * grown)).astype(BF16)], axis=1
                )
                total = log_r[:, TOKENS - 1 :]
                left = (k_t * (key_row * jnp.exp(total - log_r))).astype(BF16)
                units.append([j, coupling, eye - jnp.where(apart == 1, coupling, 0.0), right, left,
                              rate_r, total])
        size = 2
        while size < TOKENS:
            band = (apart >= size) & (apart < 2 * size)
            inverses = [unit[2].astype(BF16) for unit in units]
            inner = [
                mm(jnp.where(band, unit[1], 0.0).astype(BF16), inv).astype(BF16)
                for unit, inv in zip(units, inverses)
            ]
            for unit, inv, part in zip(units, inverses, inner):
                unit[2] = unit[2] - mm(inv, part)
            size *= 2
        spans = []
        for j, _, inverse, right, left, rate_r, total in units:
            solved = mm((inverse * rate_r).astype(BF16), right).astype(BF16)
            uw[j] = solved
            span = mm(left, solved)
            keep = eye * (1.0 - jnp.exp(total))
            spans.append(
                jnp.concatenate([span[:, :HEAD_DIM], span[:, HEAD_DIM:] + keep], axis=1).astype(BF16)
            )
        return spans

    y_copies = [
        remote(ysend.at[i], yg.at[y], ys_sem.at[i], yr_sem.at[i], y_peers[i]) for i in range(3)
    ]
    first = terms((0, 1))
    for n, span in enumerate(first):
        ysend[n // 2, n % 2] = span
    pl.semaphore_wait(barrier, 9)
    y_copies[0].start()
    y_copies[1].start()
    second = terms((2, 3))
    ysend[2, 0] = second[0]
    ysend[2, 1] = second[1]
    y_copies[2].start()
    yg[y, 0] = second[2]
    yg[y, 1] = second[3]
    for copy in y_copies:
        copy.wait_recv()

    z_copies = {}

    def z_send(e, step, up):
        slot = lax.rem(z + (NZ - step if up else step), NZ)
        n = (e * 2 + (0 if up else 1)) * 4 + step
        copy = remote(zg.at[slot, e], zg.at[slot, e], zs_sem.at[n], zr_sem.at[n],
                      z_up if up else z_down)
        copy.start()
        z_copies[e, step, up] = copy

    y_spans = [[yg[j, e].astype(F32) for j in range(NY)] for e in range(2)]
    halves = [(compose(s[1], s[0]), compose(s[3], s[2])) for s in y_spans]
    for e in range(2):
        zg[z, e] = compose(halves[e][1], halves[e][0]).astype(BF16)
    for e in range(2):
        z_send(e, 0, True)
        z_send(e, 0, False)
    for e in range(2):
        sm_spans = (y_spans[e][0], halves[e][0], compose(y_spans[e][2], halves[e][0]))
        for m in range(3):
            pairs[4 + m, e] = sm_spans[m]

    def output_terms(spots):
        for i in spots:
            for e in range(2):
                j = 2 * i + e
                part = mm(pm[j], uw[j])
                pu[j] = part[:, :HEAD_DIM]
                qg[j] = qg[j] - part[:, HEAD_DIM:]
                off = pl.multiple_of(owners[i] * 2 * HEAD_DIM + e * HEAD_DIM, HEAD_DIM)
                gate = g_ref[:, pl.ds(off, HEAD_DIM)].astype(F32)
                gated[j] = gate / (1.0 + jnp.exp(-gate)) * gain_ref[...]

    for step in range(1, 4):
        if step == 1:
            output_terms((0, 1))
        elif step == 2:
            output_terms((2, 3))
        for e in range(2):
            for up in (True, False):
                z_copies[e, step - 1, up].wait_recv()
                if step < 3 or up == (e == 0):
                    z_send(e, step, up)
    for e in range(2):
        z_copies[e, 3, e == 0].wait_recv()

    x_copies = []
    quads = []
    for e in range(2):
        z_spans = [zg[j, e].astype(F32) for j in range(NZ)]
        twos = [compose(z_spans[2 * j + 1], z_spans[2 * j]) for j in range(4)]
        fours = [compose(twos[1], twos[0]), compose(twos[3], twos[2])]
        xsend[e] = compose(fours[1], fours[0]).astype(BF16)
        for d in range(3):
            n = e * 3 + d
            copy = remote(xsend.at[e], xg.at[x, e], xs_sem.at[n], xr_sem.at[n], x_peers[d])
            copy.start()
            x_copies.append(copy)
        for j in range(4):
            pairs[j, e] = twos[j]
        quads.append(fours[0])

    ahead = []
    for e in range(2):
        b2, b1, b0 = lax.div(z, 4), lax.rem(lax.div(z, 2), 2), lax.rem(z, 2)
        quad = jnp.where(b2 == 1, quads[e], 0.0)
        two = jnp.where(b1 == 1, pairs[2 * b2, e], 0.0)
        one = jnp.where(b0 == 1, zg[4 * b2 + 2 * b1, e].astype(F32), 0.0)
        ahead.append(compose(one, compose(two, quad)))

    for e in range(2):
        for d in range(3):
            x_copies[e * 3 + d].wait_recv()
        state = jnp.where(x > 0, xg[0, e, :, :HEAD_DIM].astype(F32), 0.0)
        for j in range(1, 3):
            state = jnp.where(x > j, advance(xg[j, e].astype(F32), state), state)
        state = advance(ahead[e], state)
        sm[0, e] = state.astype(BF16)
        for m in range(3):
            sm[m + 1, e] = advance(pairs[4 + m, e], state).astype(BF16)

    back = [
        remote(sm.at[owners[i]], sin.at[y], bs_sem.at[i], br_sem.at[i], y_peers[i]) for i in range(3)
    ]
    for copy in back:
        copy.start()
    sin[y] = sm[y]
    weights.wait()
    for i in (3, 2, 1, 0):
        if i < 3:
            back[(0, 1, 2)[i]].wait_recv()
        source = (owners[0], owners[2], owners[1], y)[i]
        spot = (0, 2, 1, 3)[i]
        for e in range(2):
            j = 2 * spot + e
            o = pu[j] + mm(qg[j].astype(BF16), sin[source, e])
            inv = lax.rsqrt(jnp.mean(o * o, axis=1, keepdims=True) + EPS)
            off = pl.multiple_of(source * 2 * HEAD_DIM + e * HEAD_DIM, HEAD_DIM)
            nrm[:, pl.ds(off, HEAD_DIM)] = (o * inv * gated[j]).astype(BF16)

    half = out_ref.shape[1]
    theirs = pl.multiple_of((1 - core) * half, half)
    mine = pl.multiple_of(core * half, half)
    psend[...] = mm(nrm[...], w_vm[:, pl.ds(theirs, half)]).astype(BF16)
    swap = remote(psend, precv, ps_sem, pr_sem, partner)
    swap.start()
    own = mm(nrm[...], w_vm[:, pl.ds(mine, half)])
    swap.wait_recv()
    out_ref[...] = (own + precv[...].astype(F32)).astype(BF16)
    for copy in y_copies + list(z_copies.values()) + x_copies + back + [swap]:
        copy.wait_send()


def per_device(queries, key_rows, values, out_gate, write_rate, log_decay, norm_gain, out_weight):
    tokens = queries.shape[0]
    features = out_weight.shape[1]
    vmem = pl.BlockSpec(memory_space=pltpu.VMEM)
    heads = write_rate.shape[0]
    wide = (TOKENS, 2 * HEAD_DIM)
    square = (TOKENS, HEAD_DIM)
    dma = pltpu.SemaphoreType.DMA
    return pl.pallas_call(
        kernel,
        out_shape=jax.ShapeDtypeStruct((tokens, features // 2), BF16),
        in_specs=[vmem] * 7 + [pl.BlockSpec(memory_space=pl.ANY)],
        out_specs=vmem,
        scratch_shapes=[
            pltpu.VMEM(out_weight.shape, BF16),
            pltpu.VMEM((heads,) + wide, BF16),
            pltpu.VMEM((heads,) + square, BF16),
            pltpu.VMEM((heads,) + square, F32),
            pltpu.VMEM((heads,) + square, F32),
            pltpu.VMEM((heads,) + square, F32),
            pltpu.VMEM((3, 2) + wide, BF16),
            pltpu.VMEM((NY, 2) + wide, BF16),
            pltpu.VMEM((NZ, 2) + wide, BF16),
            pltpu.VMEM((7, 2) + wide, F32),
            pltpu.VMEM((2,) + wide, BF16),
            pltpu.VMEM((NX, 2) + wide, BF16),
            pltpu.VMEM((NY, 2) + square, BF16),
            pltpu.VMEM((NY, 2) + square, BF16),
            pltpu.VMEM((tokens, heads * HEAD_DIM), BF16),
            pltpu.VMEM((tokens, features // 2), BF16),
            pltpu.VMEM((tokens, features // 2), BF16),
            dma, dma((3,)), dma((3,)), dma((16,)), dma((16,)), dma((6,)), dma((6,)),
            dma((3,)), dma((3,)), dma, dma,
        ],
        compiler_params=pltpu.CompilerParams(
            collective_id=0, has_side_effects=True, vmem_limit_bytes=48 << 20
        ),
    )(
        queries, key_rows, values, out_gate, write_rate, log_decay,
        norm_gain.reshape(1, HEAD_DIM), out_weight,
    )


def solution(mesh):
    return jax.shard_map(
        per_device,
        mesh=mesh,
        in_specs=(
            P("seq", "head"),
            P("seq", "head"),
            P("seq", "head"),
            P("seq", "head"),
            P("head", "seq"),
            P("head", "seq"),
            P(),
            P("head", None),
        ),
        out_specs=P("seq", "head"),
        check_vma=False,
    )
```

time: 1000 us -> 58.9 us (0.06)
  waiting for transfers between devices: 691 us -> 0 us
  matrix products: 275 us -> 0 us
  Pallas kernels: 0 us -> 50 us
  between operations: 13.5 us -> 0.02 us
    all_gather x2 -> x0, waiting for transfers between devices: 678 us -> none  [carried_in(): everything = jax.tree.map(lambda part: lax.all_gather(part, axis), value)]
    dot_general x156 -> x0, matrix products: 275 us -> none  [the longest x128 242 us: combine(): jnp.einsum('hij,hjk->hik', later_pair[0], earlier[1], precision=highest)]
    pallas_call x0 -> x1, Pallas kernels: none -> 50 us  [per_device(): pl.pallas_call(kernel, out_shape=jax.ShapeDtypeStruct((tokens, features /...]
    reduce_scatter x1 -> x0, waiting for transfers between devices: 12 us -> none  [per_device(): lax.psum_scatter(partial_value.astype(jnp.bfloat16), 'head', scatter_dime...]
  transfers between devices with their start and end apart: 3 -> 0, of which waited for: 3 -> 0; matrix products, arithmetic and copies ran while one was open for 0% -> 0% of each run, Pallas kernels for 0% -> 0%
where the time goes in v1:
time: 58.9 us; the launch traced here: 58.7 us
  Pallas kernels  50 us (85%)
  local copies, waits for them, and re-layouts  8.63 us (15%)
    pallas_call x1, Pallas kernels, per_device(): pl.pallas_call(kernel, out_shape=jax.ShapeDtypeStruct((tokens, features /...  50 us
    unnamed x17, local copies, waits for them, and re-layouts  8.63 us

profile of v1, /device:TPU:1, one launch (start us, length us, event | category | flops | bytes accessed | tf_op | source)
XLA Modules:
  0.0 58.7 jit_solution(13951458018342471044)
XLA Ops:
  0.0 0.0 copy-start
  0.0 2.2 %copy-done = bf16[1024,2048]{1,0:T(8,128)(2,1)S(1)} copy-done((bf16[1024,2048]{1,0:T(8,128)(2,1)S(1)}, bf16[1024,2048]{1,0:T(8,128)(2,1)}, u32[]{:S(2)}) %copy-start) | copy-done | bytes 4194328
  2.2 0.0 copy-start.1
  2.2 0.9 %copy-done.1 = bf16[128,1024]{1,0:T(8,128)(2,1)S(1)} copy-done((bf16[128,1024]{1,0:T(8,128)(2,1)S(1)}, bf16[128,1024]{1,0:T(8,128)(2,1)}, u32[]{:S(2)}) %copy-start.1) | copy-done | bytes 262168
  3.1 0.0 copy-start.2
  3.1 0.9 %copy-done.2 = bf16[128,1024]{1,0:T(8,128)(2,1)S(1)} copy-done((bf16[128,1024]{1,0:T(8,128)(2,1)S(1)}, bf16[128,1024]{1,0:T(8,128)(2,1)}, u32[]{:S(2)}) %copy-start.2) | copy-done | bytes 262168
  4.1 0.0 copy-start.3
  4.1 0.9 %copy-done.3 = bf16[128,512]{1,0:T(8,128)(2,1)S(1)} copy-done((bf16[128,512]{1,0:T(8,128)(2,1)S(1)}, bf16[128,512]{1,0:T(8,128)(2,1)}, u32[]{:S(2)}) %copy-start.3) | copy-done | bytes 131096
  5.0 0.0 copy-start.4
  5.0 0.9 %copy-done.4 = bf16[128,512]{1,0:T(8,128)(2,1)S(1)} copy-done((bf16[128,512]{1,0:T(8,128)(2,1)S(1)}, bf16[128,512]{1,0:T(8,128)(2,1)}, u32[]{:S(2)}) %copy-start.4) | copy-done | bytes 131096
  5.9 0.0 copy-start.5
  5.9 0.7 %copy-done.5 = f32[8,128]{1,0:T(8,128)S(1)} copy-done((f32[8,128]{1,0:T(8,128)S(1)}, f32[8,128]{1,0:T(8,128)}, u32[]{:S(2)}) %copy-start.5) | copy-done | bytes 4120
  6.6 0.0 copy-start.6
  6.6 0.7 %copy-done.6 = f32[8,128]{1,0:T(8,128)S(1)} copy-done((f32[8,128]{1,0:T(8,128)S(1)}, f32[8,128]{1,0:T(8,128)}, u32[]{:S(2)}) %copy-start.6) | copy-done | bytes 4120
  7.3 0.0 copy-start.7
  7.3 0.7 %copy-done.7 = f32[128]{0:T(128)S(1)} copy-done((f32[128]{0:T(128)S(1)}, f32[128]{0:T(128)}, u32[]{:S(2)}) %copy-start.7) | copy-done | bytes 536
  7.9 50.0 %shard_map.82 = bf16[128,1024]{1,0:T(8,128)(2,1)S(1)} custom-call(bf16[128,512]{1,0:T(8,128)(2,1)S(1)} %copy-done.3, bf16[128,512]{1,0:T(8,128)(2,1)S(1)} %copy-done.4, bf16[128,1024]{1,0:T(8,128)(2,1)S(1)} %copy-done.1, bf16[128,1024]{1,0:T(8,128)(2,1)S(1)} %copy-done.2, f32[8,128]{1,0:T(8,128)S(1)} %copy-done.5, f32[8,128]{1,0:T(8,128)S(1)} %copy-done.6, ...), custom_call_target="tpu_custom_call" | custom-call | tf_op jit(solution)/shard_map/pallas_call | solution.py:269
  58.0 0.7 %copy.10 = bf16[128,1024]{1,0:T(8,128)(2,1)} copy(bf16[128,1024]{1,0:T(8,128)(2,1)S(1)} %shard_map.82) | data formatting | bytes 524288
Async XLA Ops:
  0.0 2.2 %copy-start = (bf16[1024,2048]{1,0:T(8,128)(2,1)S(1)}, bf16[1024,2048]{1,0:T(8,128)(2,1)}, u32[]{:S(2)}) copy-start(bf16[1024,2048]{1,0:T(8,128)(2,1)} %w_hbm.1) | copy-start | bytes 12582916
  2.2 0.9 %copy-start.1 = (bf16[128,1024]{1,0:T(8,128)(2,1)S(1)}, bf16[128,1024]{1,0:T(8,128)(2,1)}, u32[]{:S(2)}) copy-start(bf16[128,1024]{1,0:T(8,128)(2,1)} %v_ref.1) | copy-start | bytes 786436
  3.1 0.9 %copy-start.2 = (bf16[128,1024]{1,0:T(8,128)(2,1)S(1)}, bf16[128,1024]{1,0:T(8,128)(2,1)}, u32[]{:S(2)}) copy-start(bf16[128,1024]{1,0:T(8,128)(2,1)} %g_ref.1) | copy-start | bytes 786436
  4.1 0.9 %copy-start.3 = (bf16[128,512]{1,0:T(8,128)(2,1)S(1)}, bf16[128,512]{1,0:T(8,128)(2,1)}, u32[]{:S(2)}) copy-start(bf16[128,512]{1,0:T(8,128)(2,1)} %q_ref.1) | copy-start | bytes 393220
  5.0 0.9 %copy-start.4 = (bf16[128,512]{1,0:T(8,128)(2,1)S(1)}, bf16[128,512]{1,0:T(8,128)(2,1)}, u32[]{:S(2)}) copy-start(bf16[128,512]{1,0:T(8,128)(2,1)} %k_ref.1) | copy-start | bytes 393220
  5.9 0.7 %copy-start.5 = (f32[8,128]{1,0:T(8,128)S(1)}, f32[8,128]{1,0:T(8,128)}, u32[]{:S(2)}) copy-start(f32[8,128]{1,0:T(8,128)} %wr_ref.1) | copy-start | bytes 12292
  6.6 0.7 %copy-start.6 = (f32[8,128]{1,0:T(8,128)S(1)}, f32[8,128]{1,0:T(8,128)}, u32[]{:S(2)}) copy-start(f32[8,128]{1,0:T(8,128)} %ld_ref.1) | copy-start | bytes 12292
  7.3 0.7 %copy-start.7 = (f32[128]{0:T(128)S(1)}, f32[128]{0:T(128)}, u32[]{:S(2)}) copy-start(f32[128]{0:T(128)} %param.14) | copy-start | bytes 1540

commit v2 on v1

--- a/solution.py
+++ b/solution.py
@@ -30,9 +30,9 @@
 
 
 def kernel(
-    q_ref, k_ref, v_ref, g_ref, wr_ref, ld_ref, gain_ref, w_hbm, out_ref,
-    w_vm, uw, pm, qg, pu, gated, ysend, yg, zg, pairs, xsend, xg, sm, sin, nrm, psend, precv,
-    wsem, ys_sem, yr_sem, zs_sem, zr_sem, xs_sem, xr_sem, bs_sem, br_sem, ps_sem, pr_sem,
+    q_hbm, k_hbm, v_hbm, g_hbm, wr_hbm, ld_hbm, gain_hbm, w_hbm, out_ref,
+    q_ref, k_ref, v_ref, g_ref, wr_ref, ld_ref, gain_ref, w_vm, uw, pm, qg, pu, gated, ysend, yg, zg, pairs, xsend, xg, sm, sin, nrm, psend, precv,
+    in_sem, ys_sem, yr_sem, zs_sem, zr_sem, xs_sem, xr_sem, bs_sem, br_sem, ps_sem, pr_sem,
 ):
     me, core = lax.axis_index("seq"), lax.axis_index("head")
     y = lax.rem(me, NY)
@@ -52,8 +52,15 @@
     barrier = pltpu.get_barrier_semaphore()
     for peer in y_peers + x_peers + [z_up, z_down, partner]:
         pl.semaphore_signal(barrier, inc=1, device_id=peer, device_id_type=MESH)
-    weights = pltpu.make_async_copy(w_hbm, w_vm, wsem)
-    weights.start()
+    loads = [
+        pltpu.make_async_copy(src, dst, in_sem.at[n])
+        for n, (src, dst) in enumerate((
+            (ld_hbm, ld_ref), (wr_hbm, wr_ref), (k_hbm, k_ref), (q_hbm, q_ref), (v_hbm, v_ref),
+            (g_hbm, g_ref), (gain_hbm, gain_ref), (w_hbm, w_vm),
+        ))
+    ]
+    for load in loads:
+        load.start()
 
     def remote(src, dst, send, recv, peer):
         return pltpu.make_async_remote_copy(
@@ -67,6 +74,8 @@
     lower, strict, diag = rows >= cols, rows > cols, rows == cols
     eye = jnp.where(diag, 1.0, 0.0).astype(F32)
 
+    for load in loads[:2]:
+        load.wait()
     rate = jnp.concatenate([wr_ref[pl.ds(2 * p, 2), :] for p in owners], axis=0)
     decay = jnp.concatenate([ld_ref[pl.ds(2 * p, 2), :] for p in owners], axis=0)
     log_row = jnp.dot(
@@ -130,6 +139,8 @@
     y_copies = [
         remote(ysend.at[i], yg.at[y], ys_sem.at[i], yr_sem.at[i], y_peers[i]) for i in range(3)
     ]
+    for load in loads[2:5]:
+        load.wait()
     first = terms((0, 1))
     for n, span in enumerate(first):
         ysend[n // 2, n % 2] = span
@@ -178,6 +189,8 @@
                 gate = g_ref[:, pl.ds(off, HEAD_DIM)].astype(F32)
                 gated[j] = gate / (1.0 + jnp.exp(-gate)) * gain_ref[...]
 
+    for load in loads[5:7]:
+        load.wait()
     for step in range(1, 4):
         if step == 1:
             output_terms((0, 1))
@@ -232,7 +245,7 @@
     for copy in back:
         copy.start()
     sin[y] = sm[y]
-    weights.wait()
+    loads[7].wait()
     for i in (3, 2, 1, 0):
         if i < 3:
             back[(0, 1, 2)[i]].wait_recv()
@@ -261,7 +274,7 @@
 def per_device(queries, key_rows, values, out_gate, write_rate, log_decay, norm_gain, out_weight):
     tokens = queries.shape[0]
     features = out_weight.shape[1]
-    vmem = pl.BlockSpec(memory_space=pltpu.VMEM)
+    hbm = pl.BlockSpec(memory_space=pltpu.HBM)
     heads = write_rate.shape[0]
     wide = (TOKENS, 2 * HEAD_DIM)
     square = (TOKENS, HEAD_DIM)
@@ -269,9 +282,16 @@
     return pl.pallas_call(
         kernel,
         out_shape=jax.ShapeDtypeStruct((tokens, features // 2), BF16),
-        in_specs=[vmem] * 7 + [pl.BlockSpec(memory_space=pl.ANY)],
-        out_specs=vmem,
+        in_specs=[hbm] * 8,
+        out_specs=pl.BlockSpec(memory_space=pltpu.VMEM),
         scratch_shapes=[
+            pltpu.VMEM(queries.shape, BF16),
+            pltpu.VMEM(key_rows.shape, BF16),
+            pltpu.VMEM(values.shape, BF16),
+            pltpu.VMEM(out_gate.shape, BF16),
+            pltpu.VMEM(write_rate.shape, F32),
+            pltpu.VMEM(log_decay.shape, F32),
+            pltpu.VMEM((1, HEAD_DIM), F32),
             pltpu.VMEM(out_weight.shape, BF16),
             pltpu.VMEM((heads,) + wide, BF16),
             pltpu.VMEM((heads,) + square, BF16),
@@ -289,11 +309,11 @@
             pltpu.VMEM((tokens, heads * HEAD_DIM), BF16),
             pltpu.VMEM((tokens, features // 2), BF16),
             pltpu.VMEM((tokens, features // 2), BF16),
-            dma, dma((3,)), dma((3,)), dma((16,)), dma((16,)), dma((6,)), dma((6,)),
+            dma((8,)), dma((3,)), dma((3,)), dma((16,)), dma((16,)), dma((6,)), dma((6,)),
             dma((3,)), dma((3,)), dma, dma,
         ],
         compiler_params=pltpu.CompilerParams(
-            collective_id=0, has_side_effects=True, vmem_limit_bytes=48 << 20
+            collective_id=0, has_side_effects=True, vmem_limit_bytes=67_043_328
         ),
     )(
         queries, key_rows, values, out_gate, write_rate, log_decay,

time: 58.9 us -> 53.3 us (0.905)
  local copies, waits for them, and re-layouts: 8.63 us -> 1.67 us
  Pallas kernels: 50 us -> 51.5 us
    unnamed x17 -> x1, local copies, waits for them, and re-layouts: 8.63 us -> 1.67 us
    pallas_call x1, Pallas kernels: 50 us -> 51.5 us  [per_device(): pl.pallas_call(kernel, out_shape=jax.ShapeDtypeStruct((tokens, features /...]
where the time goes in v2:
time: 53.3 us; the launch traced here: 53.1 us
  Pallas kernels  51.5 us (97%)
  local copies, waits for them, and re-layouts  1.67 us (3%)
    pallas_call x1, Pallas kernels, per_device(): pl.pallas_call(kernel, out_shape=jax.ShapeDtypeStruct((tokens, features /...  51.5 us
    unnamed x1, local copies, waits for them, and re-layouts  1.67 us

profile of v2, /device:TPU:1, one launch (start us, length us, event | category | flops | bytes accessed | tf_op | source)
XLA Modules:
  0.0 53.1 jit_solution(16094530402645299825)
XLA Ops:
  0.0 51.5 %shard_map.82 = bf16[128,1024]{1,0:T(8,128)(2,1)} custom-call(bf16[128,512]{1,0:T(8,128)(2,1)} %q_hbm.1, bf16[128,512]{1,0:T(8,128)(2,1)} %k_hbm.1, bf16[128,1024]{1,0:T(8,128)(2,1)} %v_hbm.1, bf16[128,1024]{1,0:T(8,128)(2,1)} %g_hbm.1, f32[8,128]{1,0:T(8,128)} %wr_hbm.1, f32[8,128]{1,0:T(8,128)} %ld_hbm.1, f32[1,128]{1,0:T(1,128)} %bitcast.1, ...), custom_call_target="tpu_custom_call" | custom-call | tf_op jit(solution)/shard_map/pallas_call | solution.py:282
  51.5 1.7 %copy.10 = bf16[128,1024]{1,0:T(8,128)(2,1)} copy(bf16[128,1024]{1,0:T(8,128)(2,1)} %shard_map.82) | data formatting | bytes 524288

commit v3 on v2

--- a/solution.py
+++ b/solution.py
@@ -31,7 +31,8 @@
 
 def kernel(
     q_hbm, k_hbm, v_hbm, g_hbm, wr_hbm, ld_hbm, gain_hbm, w_hbm, out_ref,
-    q_ref, k_ref, v_ref, g_ref, wr_ref, ld_ref, gain_ref, w_vm, uw, pm, qg, pu, gated, ysend, yg, zg, pairs, xsend, xg, sm, sin, nrm, psend, precv,
+    q_ref, k_ref, v_ref, g_ref, wr_ref, ld_ref, gain_ref, w_vm, uw, pm, qg, pu, gated,
+    ysend, yg, zg, before, xsend, xg, sm, sin, nrm, psend, precv,
     in_sem, ys_sem, yr_sem, zs_sem, zr_sem, xs_sem, xr_sem, bs_sem, br_sem, ps_sem, pr_sem,
 ):
     me, core = lax.axis_index("seq"), lax.axis_index("head")
@@ -42,15 +43,20 @@
     def at(x_, z_, y_):
         return {"seq": (x_ * NZ + z_) * NY + y_}
 
-    turns = (2, 1, 3)
-    owners = [lax.rem(y + d, NY) for d in turns] + [y]
-    y_peers = [at(x, z, owner) for owner in owners[:3]]
-    x_peers = [at(lax.rem(x + d, NX), z, y) for d in turns]
-    z_up, z_down = at(x, lax.rem(z + 1, NZ), y), at(x, lax.rem(z + NZ - 1, NZ), y)
+    zp, ze = lax.div(z, 2), lax.rem(z, 2)
+    turns = (2, 1, 3, 0)
+    owners = [lax.rem(y + d, NY) for d in turns]
+    sides = [ze, 1 - ze]
+    others = [(i, f) for i in range(NY) for f in range(2) if (i, f) != (3, 0)]
+    members = {(i, f): at(x, 2 * zp + sides[f], owners[i]) for i, f in others}
+    place = 4 * ze + y
+    x_peers = [at(lax.rem(x + d, NX), z, y) for d in (2, 1, 3)]
+    z_peers = [at(x, 2 * lax.rem(zp + d, 4) + ze, y) for d in (2, 1, 3)]
     partner = {"head": 1 - core}
 
     barrier = pltpu.get_barrier_semaphore()
-    for peer in y_peers + x_peers + [z_up, z_down, partner]:
+    signalled = list(members.values()) + x_peers + z_peers + [partner]
+    for peer in signalled:
         pl.semaphore_signal(barrier, inc=1, device_id=peer, device_id_type=MESH)
     loads = [
         pltpu.make_async_copy(src, dst, in_sem.at[n])
@@ -136,47 +142,45 @@
             )
         return spans
 
-    y_copies = [
-        remote(ysend.at[i], yg.at[y], ys_sem.at[i], yr_sem.at[i], y_peers[i]) for i in range(3)
-    ]
+    def copies_of(source, target, send, recv):
+        return {
+            (i, f): remote(source(i, f), target, send.at[2 * i + f], recv.at[2 * i + f], members[i, f])
+            for i, f in others
+        }
+
+    y_copies = copies_of(
+        lambda i, f: ysend.at[i, sides[f]], yg.at[place], ys_sem, yr_sem
+    )
     for load in loads[2:5]:
         load.wait()
-    first = terms((0, 1))
-    for n, span in enumerate(first):
+    for n, span in enumerate(terms((0, 1))):
         ysend[n // 2, n % 2] = span
-    pl.semaphore_wait(barrier, 9)
-    y_copies[0].start()
-    y_copies[1].start()
-    second = terms((2, 3))
-    ysend[2, 0] = second[0]
-    ysend[2, 1] = second[1]
-    y_copies[2].start()
-    yg[y, 0] = second[2]
-    yg[y, 1] = second[3]
-    for copy in y_copies:
-        copy.wait_recv()
-
-    z_copies = {}
-
-    def z_send(e, step, up):
-        slot = lax.rem(z + (NZ - step if up else step), NZ)
-        n = (e * 2 + (0 if up else 1)) * 4 + step
-        copy = remote(zg.at[slot, e], zg.at[slot, e], zs_sem.at[n], zr_sem.at[n],
-                      z_up if up else z_down)
+    pl.semaphore_wait(barrier, len(signalled))
+    for key in ((0, 0), (0, 1), (1, 0), (1, 1)):
+        y_copies[key].start()
+    for n, span in enumerate(terms((2, 3))):
+        ysend[2 + n // 2, n % 2] = span
+    for key in ((2, 0), (2, 1), (3, 1)):
+        y_copies[key].start()
+    yg[place] = ysend[3, ze]
+    for key in others:
+        y_copies[key].wait_recv()
+
+    ones = [yg[g].astype(F32) for g in range(8)]
+    twos = [compose(ones[2 * g + 1], ones[2 * g]) for g in range(4)]
+    fours = [compose(twos[1], twos[0]), compose(twos[3], twos[2])]
+    zg[zp] = compose(fours[1], fours[0]).astype(BF16)
+    z_copies = [
+        remote(zg.at[zp], zg.at[zp], zs_sem.at[d], zr_sem.at[d], z_peers[d]) for d in range(3)
+    ]
+    for copy in z_copies:
         copy.start()
-        z_copies[e, step, up] = copy
-
-    y_spans = [[yg[j, e].astype(F32) for j in range(NY)] for e in range(2)]
-    halves = [(compose(s[1], s[0]), compose(s[3], s[2])) for s in y_spans]
-    for e in range(2):
-        zg[z, e] = compose(halves[e][1], halves[e][0]).astype(BF16)
-    for e in range(2):
-        z_send(e, 0, True)
-        z_send(e, 0, False)
-    for e in range(2):
-        sm_spans = (y_spans[e][0], halves[e][0], compose(y_spans[e][2], halves[e][0]))
-        for m in range(3):
-            pairs[4 + m, e] = sm_spans[m]
+    six = compose(twos[2], fours[0])
+    for g, span in enumerate((
+        ones[0], twos[0], compose(ones[2], twos[0]), fours[0], compose(ones[4], fours[0]), six,
+        compose(ones[6], six),
+    )):
+        before[g] = span
 
     def output_terms(spots):
         for i in spots:
@@ -191,72 +195,50 @@
 
     for load in loads[5:7]:
         load.wait()
-    for step in range(1, 4):
-        if step == 1:
-            output_terms((0, 1))
-        elif step == 2:
-            output_terms((2, 3))
-        for e in range(2):
-            for up in (True, False):
-                z_copies[e, step - 1, up].wait_recv()
-                if step < 3 or up == (e == 0):
-                    z_send(e, step, up)
-    for e in range(2):
-        z_copies[e, 3, e == 0].wait_recv()
-
-    x_copies = []
-    quads = []
-    for e in range(2):
-        z_spans = [zg[j, e].astype(F32) for j in range(NZ)]
-        twos = [compose(z_spans[2 * j + 1], z_spans[2 * j]) for j in range(4)]
-        fours = [compose(twos[1], twos[0]), compose(twos[3], twos[2])]
-        xsend[e] = compose(fours[1], fours[0]).astype(BF16)
-        for d in range(3):
-            n = e * 3 + d
-            copy = remote(xsend.at[e], xg.at[x, e], xs_sem.at[n], xr_sem.at[n], x_peers[d])
-            copy.start()
-            x_copies.append(copy)
-        for j in range(4):
-            pairs[j, e] = twos[j]
-        quads.append(fours[0])
-
-    ahead = []
-    for e in range(2):
-        b2, b1, b0 = lax.div(z, 4), lax.rem(lax.div(z, 2), 2), lax.rem(z, 2)
-        quad = jnp.where(b2 == 1, quads[e], 0.0)
-        two = jnp.where(b1 == 1, pairs[2 * b2, e], 0.0)
-        one = jnp.where(b0 == 1, zg[4 * b2 + 2 * b1, e].astype(F32), 0.0)
-        ahead.append(compose(one, compose(two, quad)))
-
-    for e in range(2):
-        for d in range(3):
-            x_copies[e * 3 + d].wait_recv()
-        state = jnp.where(x > 0, xg[0, e, :, :HEAD_DIM].astype(F32), 0.0)
-        for j in range(1, 3):
-            state = jnp.where(x > j, advance(xg[j, e].astype(F32), state), state)
-        state = advance(ahead[e], state)
-        sm[0, e] = state.astype(BF16)
-        for m in range(3):
-            sm[m + 1, e] = advance(pairs[4 + m, e], state).astype(BF16)
-
-    back = [
-        remote(sm.at[owners[i]], sin.at[y], bs_sem.at[i], br_sem.at[i], y_peers[i]) for i in range(3)
+    output_terms(range(NY))
+    for copy in z_copies:
+        copy.wait_recv()
+
+    z_spans = [zg[j].astype(F32) for j in range(4)]
+    first_two = compose(z_spans[1], z_spans[0])
+    xsend[...] = compose(compose(z_spans[3], z_spans[2]), first_two).astype(BF16)
+    x_copies = [
+        remote(xsend, xg.at[x], xs_sem.at[d], xr_sem.at[d], x_peers[d]) for d in range(3)
     ]
-    for copy in back:
+    for copy in x_copies:
         copy.start()
-    sin[y] = sm[y]
+    b1, b0 = lax.div(zp, 2), lax.rem(zp, 2)
+    ahead = compose(
+        jnp.where(b0 == 1, zg[2 * b1].astype(F32), 0.0), jnp.where(b1 == 1, first_two, 0.0)
+    )
+    for copy in x_copies:
+        copy.wait_recv()
+    state = jnp.where(x > 0, xg[0, :, :HEAD_DIM].astype(F32), 0.0)
+    for j in range(1, 3):
+        state = jnp.where(x > j, advance(xg[j].astype(F32), state), state)
+    state = advance(ahead, state)
+    sm[0] = state.astype(BF16)
+    for g in range(7):
+        sm[g + 1] = advance(before[g], state).astype(BF16)
+
+    back = copies_of(
+        lambda i, f: sm.at[4 * sides[f] + owners[i]], sin.at[2 * y + ze], bs_sem, br_sem
+    )
+    for i in (0, 1, 2, 3):
+        for f in range(2):
+            if (i, f) in back:
+                back[i, f].start()
+    sin[2 * y + ze] = sm[place]
     loads[7].wait()
-    for i in (3, 2, 1, 0):
-        if i < 3:
-            back[(0, 1, 2)[i]].wait_recv()
-        source = (owners[0], owners[2], owners[1], y)[i]
+    for i, f in ((3, 0), (3, 1), (1, 0), (2, 0), (1, 1), (2, 1), (0, 0), (0, 1)):
+        if (i, f) in back:
+            back[i, f].wait_recv()
         spot = (0, 2, 1, 3)[i]
-        for e in range(2):
-            j = 2 * spot + e
-            o = pu[j] + mm(qg[j].astype(BF16), sin[source, e])
-            inv = lax.rsqrt(jnp.mean(o * o, axis=1, keepdims=True) + EPS)
-            off = pl.multiple_of(source * 2 * HEAD_DIM + e * HEAD_DIM, HEAD_DIM)
-            nrm[:, pl.ds(off, HEAD_DIM)] = (o * inv * gated[j]).astype(BF16)
+        j = 2 * spot + sides[f]
+        o = pu[j] + mm(qg[j].astype(BF16), sin[2 * owners[spot] + sides[f]])
+        inv = lax.rsqrt(jnp.mean(o * o, axis=1, keepdims=True) + EPS)
+        off = pl.multiple_of((2 * owners[spot] + sides[f]) * HEAD_DIM, HEAD_DIM)
+        nrm[:, pl.ds(off, HEAD_DIM)] = (o * inv * gated[j]).astype(BF16)
 
     half = out_ref.shape[1]
     theirs = pl.multiple_of((1 - core) * half, half)
@@ -267,7 +249,7 @@
     own = mm(nrm[...], w_vm[:, pl.ds(mine, half)])
     swap.wait_recv()
     out_ref[...] = (own + precv[...].astype(F32)).astype(BF16)
-    for copy in y_copies + list(z_copies.values()) + x_copies + back + [swap]:
+    for copy in list(y_copies.values()) + z_copies + x_copies + list(back.values()) + [swap]:
         copy.wait_send()
 
 
@@ -298,19 +280,19 @@
             pltpu.VMEM((heads,) + square, F32),
             pltpu.VMEM((heads,) + square, F32),
             pltpu.VMEM((heads,) + square, F32),
-            pltpu.VMEM((3, 2) + wide, BF16),
             pltpu.VMEM((NY, 2) + wide, BF16),
-            pltpu.VMEM((NZ, 2) + wide, BF16),
-            pltpu.VMEM((7, 2) + wide, F32),
-            pltpu.VMEM((2,) + wide, BF16),
-            pltpu.VMEM((NX, 2) + wide, BF16),
-            pltpu.VMEM((NY, 2) + square, BF16),
-            pltpu.VMEM((NY, 2) + square, BF16),
+            pltpu.VMEM((8,) + wide, BF16),
+            pltpu.VMEM((4,) + wide, BF16),
+            pltpu.VMEM((7,) + wide, F32),
+            pltpu.VMEM(wide, BF16),
+            pltpu.VMEM((NX,) + wide, BF16),
+            pltpu.VMEM((8,) + square, BF16),
+            pltpu.VMEM((8,) + square, BF16),
             pltpu.VMEM((tokens, heads * HEAD_DIM), BF16),
             pltpu.VMEM((tokens, features // 2), BF16),
             pltpu.VMEM((tokens, features // 2), BF16),
-            dma((8,)), dma((3,)), dma((3,)), dma((16,)), dma((16,)), dma((6,)), dma((6,)),
-            dma((3,)), dma((3,)), dma, dma,
+            dma((8,)), dma((8,)), dma((8,)), dma((3,)), dma((3,)), dma((3,)), dma((3,)),
+            dma((8,)), dma((8,)), dma, dma,
         ],
         compiler_params=pltpu.CompilerParams(
             collective_id=0, has_side_effects=True, vmem_limit_bytes=67_043_328

time: 53.3 us -> 45.1 us (0.85)
  Pallas kernels: 51.5 us -> 43.4 us
    pallas_call x1, Pallas kernels: 51.5 us -> 43.4 us  [per_device(): pl.pallas_call(kernel, out_shape=jax.ShapeDtypeStruct((tokens, features /...]
where the time goes in v3:
time: 45.1 us; the launch traced here: 45 us
  Pallas kernels  43.4 us (96%)
  local copies, waits for them, and re-layouts  1.67 us (4%)
    pallas_call x1, Pallas kernels, per_device(): pl.pallas_call(kernel, out_shape=jax.ShapeDtypeStruct((tokens, features /...  43.4 us
    unnamed x1, local copies, waits for them, and re-layouts  1.67 us

profile of v3, /device:TPU:1, one launch (start us, length us, event | category | flops | bytes accessed | tf_op | source)
XLA Modules:
  0.0 45.0 jit_solution(6691107914233603854)
XLA Ops:
  0.0 43.4 %shard_map.82 = bf16[128,1024]{1,0:T(8,128)(2,1)} custom-call(bf16[128,512]{1,0:T(8,128)(2,1)} %q_hbm.1, bf16[128,512]{1,0:T(8,128)(2,1)} %k_hbm.1, bf16[128,1024]{1,0:T(8,128)(2,1)} %v_hbm.1, bf16[128,1024]{1,0:T(8,128)(2,1)} %g_hbm.1, f32[8,128]{1,0:T(8,128)} %wr_hbm.1, f32[8,128]{1,0:T(8,128)} %ld_hbm.1, f32[1,128]{1,0:T(1,128)} %bitcast.1, ...), custom_call_target="tpu_custom_call" | custom-call | tf_op jit(solution)/shard_map/pallas_call | solution.py:264
  43.4 1.7 %copy.10 = bf16[128,1024]{1,0:T(8,128)(2,1)} copy(bf16[128,1024]{1,0:T(8,128)(2,1)} %shard_map.82) | data formatting | bytes 524288

commit v4 on v3

--- a/solution.py
+++ b/solution.py
@@ -31,33 +31,10 @@
 
 def kernel(
     q_hbm, k_hbm, v_hbm, g_hbm, wr_hbm, ld_hbm, gain_hbm, w_hbm, out_ref,
-    q_ref, k_ref, v_ref, g_ref, wr_ref, ld_ref, gain_ref, w_vm, uw, pm, qg, pu, gated,
+    q_ref, k_ref, v_ref, g_ref, wr_ref, ld_ref, gain_ref, w_vm, key_rows, uw, qe, pu, gated,
     ysend, yg, zg, before, xsend, xg, sm, sin, nrm, psend, precv,
     in_sem, ys_sem, yr_sem, zs_sem, zr_sem, xs_sem, xr_sem, bs_sem, br_sem, ps_sem, pr_sem,
 ):
-    me, core = lax.axis_index("seq"), lax.axis_index("head")
-    y = lax.rem(me, NY)
-    z = lax.rem(lax.div(me, NY), NZ)
-    x = lax.div(me, NY * NZ)
-
-    def at(x_, z_, y_):
-        return {"seq": (x_ * NZ + z_) * NY + y_}
-
-    zp, ze = lax.div(z, 2), lax.rem(z, 2)
-    turns = (2, 1, 3, 0)
-    owners = [lax.rem(y + d, NY) for d in turns]
-    sides = [ze, 1 - ze]
-    others = [(i, f) for i in range(NY) for f in range(2) if (i, f) != (3, 0)]
-    members = {(i, f): at(x, 2 * zp + sides[f], owners[i]) for i, f in others}
-    place = 4 * ze + y
-    x_peers = [at(lax.rem(x + d, NX), z, y) for d in (2, 1, 3)]
-    z_peers = [at(x, 2 * lax.rem(zp + d, 4) + ze, y) for d in (2, 1, 3)]
-    partner = {"head": 1 - core}
-
-    barrier = pltpu.get_barrier_semaphore()
-    signalled = list(members.values()) + x_peers + z_peers + [partner]
-    for peer in signalled:
-        pl.semaphore_signal(barrier, inc=1, device_id=peer, device_id_type=MESH)
     loads = [
         pltpu.make_async_copy(src, dst, in_sem.at[n])
         for n, (src, dst) in enumerate((
@@ -68,6 +45,30 @@
     for load in loads:
         load.start()
 
+    me, core = lax.axis_index("seq"), lax.axis_index("head")
+    y = lax.rem(me, NY)
+    z = lax.rem(lax.div(me, NY), NZ)
+    x = lax.div(me, NY * NZ)
+
+    def at(x_, z_, y_):
+        return {"seq": (x_ * NZ + z_) * NY + y_}
+
+    zp, ze = lax.div(z, 2), lax.rem(z, 2)
+    turns = (2, 1, 3, 0)
+    owners = [lax.rem(y + d, NY) for d in turns]
+    sides = [ze, 1 - ze]
+    others = [(i, f) for i in range(NY) for f in range(2) if (i, f) != (3, 0)]
+    members = {(i, f): at(x, 2 * zp + sides[f], owners[i]) for i, f in others}
+    place = 4 * ze + y
+    x_turns = (2, 1, 3)
+    x_peers = [at(lax.rem(x + d, NX), z, y) for d in x_turns]
+    z_peers = [at(x, 2 * lax.rem(zp + d, 4) + ze, y) for d in (2, 1, 3)]
+    partner = {"head": 1 - core}
+
+    barrier = pltpu.get_barrier_semaphore()
+    signalled = list(members.values()) + x_peers + z_peers + [partner]
+    for peer in signalled:
+        pl.semaphore_signal(barrier, inc=1, device_id=peer, device_id_type=MESH)
     def remote(src, dst, send, recv, peer):
         return pltpu.make_async_remote_copy(
             src_ref=src, dst_ref=dst, send_sem=send, recv_sem=recv,
@@ -94,14 +95,13 @@
         units = []
         for i in spots:
             off = pl.multiple_of(owners[i] * HEAD_DIM, HEAD_DIM)
-            kb, qb = k_ref[:, pl.ds(off, HEAD_DIM)], q_ref[:, pl.ds(off, HEAD_DIM)]
-            kf, qf = kb.astype(F32), qb.astype(F32)
-            dots = mm_nt(jnp.concatenate([kb, qb], axis=0), kb)
-            key_dots, query_dots = dots[:TOKENS], dots[TOKENS:]
+            kb = k_ref[:, pl.ds(off, HEAD_DIM)]
+            kf = kb.astype(F32)
+            key_dots = mm_nt(kb, kb)
             key_row = lax.rsqrt(jnp.sum(jnp.where(diag, key_dots, 0.0), axis=0, keepdims=True) + EPS)
             key_col = lax.rsqrt(jnp.sum(kf * kf, axis=1, keepdims=True) + EPS)
-            query_col = lax.rsqrt(jnp.sum(qf * qf, axis=1, keepdims=True) + EPS) * HEAD_DIM**-0.5
-            key_dots, query_dots = key_dots * key_row, query_dots * key_row
+            key_dots = key_dots * key_row
+            key_rows[i : i + 1, :] = key_row
             k_t = kf.T
             for e in range(2):
                 j = 2 * i + e
@@ -110,8 +110,6 @@
                 fade = jnp.exp(jnp.minimum(log_c - log_r, 0.0))
                 grown = jnp.exp(log_c)
                 coupling = jnp.where(strict, key_dots * fade * (rate_c * key_col), 0.0)
-                pm[j] = jnp.where(lower, query_dots * fade * query_col, 0.0).astype(BF16)
-                qg[j] = qf * (query_col * grown)
                 v_off = pl.multiple_of(owners[i] * 2 * HEAD_DIM + e * HEAD_DIM, HEAD_DIM)
                 right = jnp.concatenate(
                     [v_ref[:, pl.ds(v_off, HEAD_DIM)], (kf * (key_col * grown)).astype(BF16)], axis=1
@@ -184,11 +182,19 @@
 
     def output_terms(spots):
         for i in spots:
+            off = pl.multiple_of(owners[i] * HEAD_DIM, HEAD_DIM)
+            kb, qb = k_ref[:, pl.ds(off, HEAD_DIM)], q_ref[:, pl.ds(off, HEAD_DIM)]
+            qf = qb.astype(F32)
+            query_col = lax.rsqrt(jnp.sum(qf * qf, axis=1, keepdims=True) + EPS) * HEAD_DIM**-0.5
+            query_dots = mm_nt(qb, kb) * key_rows[i : i + 1, :] * query_col
             for e in range(2):
                 j = 2 * i + e
-                part = mm(pm[j], uw[j])
+                log_r, log_c = log_row[j : j + 1, :], columns[:, j : j + 1]
+                fade = jnp.exp(jnp.minimum(log_c - log_r, 0.0))
+                scores = jnp.where(lower, query_dots * fade, 0.0).astype(BF16)
+                part = mm(scores, uw[j])
                 pu[j] = part[:, :HEAD_DIM]
-                qg[j] = qg[j] - part[:, HEAD_DIM:]
+                qe[j] = (qf * (query_col * jnp.exp(log_c)) - part[:, HEAD_DIM:]).astype(BF16)
                 off = pl.multiple_of(owners[i] * 2 * HEAD_DIM + e * HEAD_DIM, HEAD_DIM)
                 gate = g_ref[:, pl.ds(off, HEAD_DIM)].astype(F32)
                 gated[j] = gate / (1.0 + jnp.exp(-gate)) * gain_ref[...]
@@ -205,14 +211,14 @@
     x_copies = [
         remote(xsend, xg.at[x], xs_sem.at[d], xr_sem.at[d], x_peers[d]) for d in range(3)
     ]
-    for copy in x_copies:
-        copy.start()
+    for turn, copy in zip(x_turns, x_copies):
+        pl.when(x + turn < NX)(copy.start)
     b1, b0 = lax.div(zp, 2), lax.rem(zp, 2)
     ahead = compose(
         jnp.where(b0 == 1, zg[2 * b1].astype(F32), 0.0), jnp.where(b1 == 1, first_two, 0.0)
     )
-    for copy in x_copies:
-        copy.wait_recv()
+    for turn, copy in zip(x_turns, x_copies):
+        pl.when(x >= turn)(copy.wait_recv)
     state = jnp.where(x > 0, xg[0, :, :HEAD_DIM].astype(F32), 0.0)
     for j in range(1, 3):
         state = jnp.where(x > j, advance(xg[j].astype(F32), state), state)
@@ -235,7 +241,7 @@
             back[i, f].wait_recv()
         spot = (0, 2, 1, 3)[i]
         j = 2 * spot + sides[f]
-        o = pu[j] + mm(qg[j].astype(BF16), sin[2 * owners[spot] + sides[f]])
+        o = pu[j] + mm(qe[j], sin[2 * owners[spot] + sides[f]])
         inv = lax.rsqrt(jnp.mean(o * o, axis=1, keepdims=True) + EPS)
         off = pl.multiple_of((2 * owners[spot] + sides[f]) * HEAD_DIM, HEAD_DIM)
         nrm[:, pl.ds(off, HEAD_DIM)] = (o * inv * gated[j]).astype(BF16)
@@ -249,7 +255,9 @@
     own = mm(nrm[...], w_vm[:, pl.ds(mine, half)])
     swap.wait_recv()
     out_ref[...] = (own + precv[...].astype(F32)).astype(BF16)
-    for copy in list(y_copies.values()) + z_copies + x_copies + list(back.values()) + [swap]:
+    for turn, copy in zip(x_turns, x_copies):
+        pl.when(x + turn < NX)(copy.wait_send)
+    for copy in list(y_copies.values()) + z_copies + list(back.values()) + [swap]:
         copy.wait_send()
 
 
@@ -275,9 +283,9 @@
             pltpu.VMEM(log_decay.shape, F32),
             pltpu.VMEM((1, HEAD_DIM), F32),
             pltpu.VMEM(out_weight.shape, BF16),
+            pltpu.VMEM((8, TOKENS), F32),
             pltpu.VMEM((heads,) + wide, BF16),
             pltpu.VMEM((heads,) + square, BF16),
-            pltpu.VMEM((heads,) + square, F32),
             pltpu.VMEM((heads,) + square, F32),
             pltpu.VMEM((heads,) + square, F32),
             pltpu.VMEM((NY, 2) + wide, BF16),
@@ -295,12 +303,15 @@
             dma((8,)), dma((8,)), dma, dma,
         ],
         compiler_params=pltpu.CompilerParams(
-            collective_id=0, has_side_effects=True, vmem_limit_bytes=67_043_328
+            collective_id=0, has_side_effects=True, vmem_limit_bytes=48 << 20
         ),
-    )(
-        queries, key_rows, values, out_gate, write_rate, log_decay,
-        norm_gain.reshape(1, HEAD_DIM), out_weight,
-    )
+    )(*(
+        pltpu.with_memory_space_constraint(operand, pltpu.HBM)
+        for operand in (
+            queries, key_rows, values, out_gate, write_rate, log_decay,
+            norm_gain.reshape(1, HEAD_DIM), out_weight,
+        )
+    ))
 
 
 def solution(mesh):

time: 45.1 us -> 40.4 us (0.90)
  the two profiles are of different devices: /device:TPU:1 before, /device:TPU:7 now
where the time goes in v4:
time: 40.4 us; the launch traced here: 40.3 us
  Pallas kernels  39.6 us (98%)
  local copies, waits for them, and re-layouts  0.71 us (2%)
    pallas_call x1, Pallas kernels, per_device(): pl.pallas_call(kernel, out_shape=jax.ShapeDtypeStruct((tokens, features /...  39.6 us

profile of v4, /device:TPU:7, one launch (start us, length us, event | category | flops | bytes accessed | tf_op | source)
XLA Modules:
  0.0 40.3 jit_solution(398964928297337945)
XLA Ops:
  0.0 39.6 %shard_map.82 = bf16[128,1024]{1,0:T(8,128)(2,1)S(1)} custom-call(bf16[128,512]{1,0:T(8,128)(2,1)} %q_hbm.1, bf16[128,512]{1,0:T(8,128)(2,1)} %k_hbm.1, bf16[128,1024]{1,0:T(8,128)(2,1)} %v_hbm.1, bf16[128,1024]{1,0:T(8,128)(2,1)} %g_hbm.1, f32[8,128]{1,0:T(8,128)} %wr_hbm.1, f32[8,128]{1,0:T(8,128)} %ld_hbm.1, f32[1,128]{1,0:T(1,128)} %bitcast.1, ...), custom_call_target="tpu_custom_call" | custom-call | tf_op jit(solution)/shard_map/pallas_call | solution.py:272
  39.6 0.7 %copy.10 = bf16[128,1024]{1,0:T(8,128)(2,1)} copy(bf16[128,1024]{1,0:T(8,128)(2,1)S(1)} %shard_map.82) | data formatting | bytes 524288

commit v5 on v4

--- a/solution.py
+++ b/solution.py
@@ -32,7 +32,7 @@
 def kernel(
     q_hbm, k_hbm, v_hbm, g_hbm, wr_hbm, ld_hbm, gain_hbm, w_hbm, out_ref,
     q_ref, k_ref, v_ref, g_ref, wr_ref, ld_ref, gain_ref, w_vm, key_rows, uw, qe, pu, gated,
-    ysend, yg, zg, before, xsend, xg, sm, sin, nrm, psend, precv,
+    ysend, yg, zg, before, xsend, xg, sm, sin, to_them, own, psend, precv,
     in_sem, ys_sem, yr_sem, zs_sem, zr_sem, xs_sem, xr_sem, bs_sem, br_sem, ps_sem, pr_sem,
 ):
     loads = [
@@ -118,17 +118,24 @@
                 left = (k_t * (key_row * jnp.exp(total - log_r))).astype(BF16)
                 units.append([j, coupling, eye - jnp.where(apart == 1, coupling, 0.0), right, left,
                               rate_r, total])
-        size = 2
-        while size < TOKENS:
-            band = (apart >= size) & (apart < 2 * size)
+        for size in (2, 8, 32):
+            band = (apart >= size) & (apart < 4 * size)
             inverses = [unit[2].astype(BF16) for unit in units]
-            inner = [
+            steps = [
                 mm(jnp.where(band, unit[1], 0.0).astype(BF16), inv).astype(BF16)
                 for unit, inv in zip(units, inverses)
             ]
-            for unit, inv, part in zip(units, inverses, inner):
-                unit[2] = unit[2] - mm(inv, part)
-            size *= 2
+            squares = [
+                mm(jnp.concatenate([step, inv], axis=0), step) for step, inv in zip(steps, inverses)
+            ]
+            for unit, square in zip(units, squares):
+                unit[2] = unit[2] - square[TOKENS:]
+            more = [
+                mm(unit[2].astype(BF16), square[:TOKENS].astype(BF16))
+                for unit, square in zip(units, squares)
+            ]
+            for unit, part in zip(units, more):
+                unit[2] = unit[2] + part
         spans = []
         for j, _, inverse, right, left, rate_r, total in units:
             solved = mm((inverse * rate_r).astype(BF16), right).astype(BF16)
@@ -217,13 +224,14 @@
     ahead = compose(
         jnp.where(b0 == 1, zg[2 * b1].astype(F32), 0.0), jnp.where(b1 == 1, first_two, 0.0)
     )
+    for g in range(7):
+        before[g] = compose(before[g], ahead)
     for turn, copy in zip(x_turns, x_copies):
         pl.when(x >= turn)(copy.wait_recv)
     state = jnp.where(x > 0, xg[0, :, :HEAD_DIM].astype(F32), 0.0)
     for j in range(1, 3):
         state = jnp.where(x > j, advance(xg[j].astype(F32), state), state)
-    state = advance(ahead, state)
-    sm[0] = state.astype(BF16)
+    sm[0] = advance(ahead, state).astype(BF16)
     for g in range(7):
         sm[g + 1] = advance(before[g], state).astype(BF16)
 
@@ -236,28 +244,47 @@
                 back[i, f].start()
     sin[2 * y + ze] = sm[place]
     loads[7].wait()
-    for i, f in ((3, 0), (3, 1), (1, 0), (2, 0), (1, 1), (2, 1), (0, 0), (0, 1)):
+    def normed(i, f):
         if (i, f) in back:
             back[i, f].wait_recv()
         spot = (0, 2, 1, 3)[i]
         j = 2 * spot + sides[f]
         o = pu[j] + mm(qe[j], sin[2 * owners[spot] + sides[f]])
         inv = lax.rsqrt(jnp.mean(o * o, axis=1, keepdims=True) + EPS)
-        off = pl.multiple_of((2 * owners[spot] + sides[f]) * HEAD_DIM, HEAD_DIM)
-        nrm[:, pl.ds(off, HEAD_DIM)] = (o * inv * gated[j]).astype(BF16)
+        out = (o * inv * gated[j]).astype(BF16)
+        row = pl.multiple_of((2 * owners[spot] + sides[f]) * HEAD_DIM, HEAD_DIM)
+        return out, row
 
     half = out_ref.shape[1]
     theirs = pl.multiple_of((1 - core) * half, half)
     mine = pl.multiple_of(core * half, half)
-    psend[...] = mm(nrm[...], w_vm[:, pl.ds(theirs, half)]).astype(BF16)
-    swap = remote(psend, precv, ps_sem, pr_sem, partner)
-    swap.start()
-    own = mm(nrm[...], w_vm[:, pl.ds(mine, half)])
-    swap.wait_recv()
-    out_ref[...] = (own + precv[...].astype(F32)).astype(BF16)
+
+    def project(parts, first, count):
+        left = jnp.concatenate([out for out, _ in parts], axis=1)
+        return mm(left, jnp.concatenate(
+            [w_vm[pl.ds(row, HEAD_DIM), pl.ds(first, count)] for _, row in parts], axis=0))
+
+    parts = [normed(i, f) for i, f in ((3, 0), (3, 1), (1, 0), (2, 0), (1, 1), (2, 1))]
+    to_them[...] = project(parts, theirs, half)
+    own[...] = project(parts, mine, half)
+    parts = [normed(0, 0), normed(0, 1)]
+    swaps = []
+    for n in range(2):
+        psend[n] = (
+            to_them[:, n * (half // 2) : (n + 1) * (half // 2)]
+            + project(parts, pl.multiple_of(theirs + n * (half // 2), half // 2), half // 2)
+        ).astype(BF16)
+        swap = remote(psend.at[n], precv.at[n], ps_sem.at[n], pr_sem.at[n], partner)
+        swap.start()
+        swaps.append(swap)
+    own[...] = own[...] + project(parts, mine, half)
+    for n, swap in enumerate(swaps):
+        swap.wait_recv()
+        piece = pl.ds(n * (half // 2), half // 2)
+        out_ref[:, piece] = (own[:, piece] + precv[n].astype(F32)).astype(BF16)
     for turn, copy in zip(x_turns, x_copies):
         pl.when(x + turn < NX)(copy.wait_send)
-    for copy in list(y_copies.values()) + z_copies + list(back.values()) + [swap]:
+    for copy in list(y_copies.values()) + z_copies + list(back.values()) + swaps:
         copy.wait_send()
 
 
@@ -296,11 +323,12 @@
             pltpu.VMEM((NX,) + wide, BF16),
             pltpu.VMEM((8,) + square, BF16),
             pltpu.VMEM((8,) + square, BF16),
-            pltpu.VMEM((tokens, heads * HEAD_DIM), BF16),
-            pltpu.VMEM((tokens, features // 2), BF16),
-            pltpu.VMEM((tokens, features // 2), BF16),
+            pltpu.VMEM((tokens, features // 2), F32),
+            pltpu.VMEM((tokens, features // 2), F32),
+            pltpu.VMEM((2, tokens, features // 4), BF16),
+            pltpu.VMEM((2, tokens, features // 4), BF16),
             dma((8,)), dma((8,)), dma((8,)), dma((3,)), dma((3,)), dma((3,)), dma((3,)),
-            dma((8,)), dma((8,)), dma, dma,
+            dma((8,)), dma((8,)), dma((2,)), dma((2,)),
         ],
         compiler_params=pltpu.CompilerParams(
             collective_id=0, has_side_effects=True, vmem_limit_bytes=48 << 20

time: 40.4 us -> 39 us (0.965)
  Pallas kernels: 39.6 us -> 38.2 us
    pallas_call x1, Pallas kernels: 39.6 us -> 38.2 us  [per_device(): pl.pallas_call(kernel, out_shape=jax.ShapeDtypeStruct((tokens, features /...]
where the time goes in v5:
time: 39 us; the launch traced here: 38.9 us
  Pallas kernels  38.2 us (98%)
  local copies, waits for them, and re-layouts  0.71 us (2%)
    pallas_call x1, Pallas kernels, per_device(): pl.pallas_call(kernel, out_shape=jax.ShapeDtypeStruct((tokens, features /...  38.2 us

profile of v5, /device:TPU:7, one launch (start us, length us, event | category | flops | bytes accessed | tf_op | source)
XLA Modules:
  0.0 38.9 jit_solution(5440518878772477829)
XLA Ops:
  0.0 38.2 %shard_map.82 = bf16[128,1024]{1,0:T(8,128)(2,1)S(1)} custom-call(bf16[128,512]{1,0:T(8,128)(2,1)} %q_hbm.1, bf16[128,512]{1,0:T(8,128)(2,1)} %k_hbm.1, bf16[128,1024]{1,0:T(8,128)(2,1)} %v_hbm.1, bf16[128,1024]{1,0:T(8,128)(2,1)} %g_hbm.1, f32[8,128]{1,0:T(8,128)} %wr_hbm.1, f32[8,128]{1,0:T(8,128)} %ld_hbm.1, f32[1,128]{1,0:T(1,128)} %bitcast.1, ...), custom_call_target="tpu_custom_call" | custom-call | tf_op jit(solution)/shard_map/pallas_call | solution.py:299
  38.2 0.7 %copy.10 = bf16[128,1024]{1,0:T(8,128)(2,1)} copy(bf16[128,1024]{1,0:T(8,128)(2,1)S(1)} %shard_map.82) | data formatting | bytes 524288

commit v6 on v5

--- a/solution.py
+++ b/solution.py
@@ -218,16 +218,23 @@
     x_copies = [
         remote(xsend, xg.at[x], xs_sem.at[d], xr_sem.at[d], x_peers[d]) for d in range(3)
     ]
-    for turn, copy in zip(x_turns, x_copies):
-        pl.when(x + turn < NX)(copy.start)
+    feed = pl.ds(0, HEAD_DIM)
+    x_feeds = [
+        remote(xsend.at[:, feed], xg.at[x, :, feed], xs_sem.at[d], xr_sem.at[d], x_peers[d])
+        for d in range(3)
+    ]
+    for turn, copy, short in zip(x_turns, x_copies, x_feeds):
+        pl.when((x > 0) & (x + turn < NX))(copy.start)
+        pl.when(x == 0)(short.start)
     b1, b0 = lax.div(zp, 2), lax.rem(zp, 2)
     ahead = compose(
         jnp.where(b0 == 1, zg[2 * b1].astype(F32), 0.0), jnp.where(b1 == 1, first_two, 0.0)
     )
     for g in range(7):
         before[g] = compose(before[g], ahead)
-    for turn, copy in zip(x_turns, x_copies):
-        pl.when(x >= turn)(copy.wait_recv)
+    for turn, copy, short in zip(x_turns, x_copies, x_feeds):
+        pl.when(x > turn)(copy.wait_recv)
+        pl.when(x == turn)(short.wait_recv)
     state = jnp.where(x > 0, xg[0, :, :HEAD_DIM].astype(F32), 0.0)
     for j in range(1, 3):
         state = jnp.where(x > j, advance(xg[j].astype(F32), state), state)
@@ -282,8 +289,9 @@
         swap.wait_recv()
         piece = pl.ds(n * (half // 2), half // 2)
         out_ref[:, piece] = (own[:, piece] + precv[n].astype(F32)).astype(BF16)
-    for turn, copy in zip(x_turns, x_copies):
-        pl.when(x + turn < NX)(copy.wait_send)
+    for turn, copy, short in zip(x_turns, x_copies, x_feeds):
+        pl.when((x > 0) & (x + turn < NX))(copy.wait_send)
+        pl.when(x == 0)(short.wait_send)
     for copy in list(y_copies.values()) + z_copies + list(back.values()) + swaps:
         copy.wait_send()
 

time: 39 us -> 39 us (level)
  no operation moved by 1% of the time
where the time goes in v6:
time: 39 us; the launch traced here: 38.9 us
  Pallas kernels  38.2 us (98%)
  local copies, waits for them, and re-layouts  0.71 us (2%)
    pallas_call x1, Pallas kernels, per_device(): pl.pallas_call(kernel, out_shape=jax.ShapeDtypeStruct((tokens, features /...  38.2 us

profile of v6, /device:TPU:7, one launch (start us, length us, event | category | flops | bytes accessed | tf_op | source)
XLA Modules:
  0.0 38.9 jit_solution(11876404146959671627)
XLA Ops:
  0.0 38.2 %shard_map.82 = bf16[128,1024]{1,0:T(8,128)(2,1)S(1)} custom-call(bf16[128,512]{1,0:T(8,128)(2,1)} %q_hbm.1, bf16[128,512]{1,0:T(8,128)(2,1)} %k_hbm.1, bf16[128,1024]{1,0:T(8,128)(2,1)} %v_hbm.1, bf16[128,1024]{1,0:T(8,128)(2,1)} %g_hbm.1, f32[8,128]{1,0:T(8,128)} %wr_hbm.1, f32[8,128]{1,0:T(8,128)} %ld_hbm.1, f32[1,128]{1,0:T(1,128)} %bitcast.1, ...), custom_call_target="tpu_custom_call" | custom-call | tf_op jit(solution)/shard_map/pallas_call | solution.py:307
  38.2 0.7 %copy.10 = bf16[128,1024]{1,0:T(8,128)(2,1)} copy(bf16[128,1024]{1,0:T(8,128)(2,1)S(1)} %shard_map.82) | data formatting | bytes 524288
